TPU v7x, 256 devices: a whole 4x4x8 slice. The times are simulated.
256 devices in a mesh: tm: 32 (over x, y, core), ens: 8 (over z).
Axes of the slice: x: 4, y: 4, z: 8, core: 2. Of those that a mesh axis runs over, the one named last changes fastest.
Arguments:
- propagators: float32 [8, 32, 512, 512], P('ens', 'tm'), may hold values from -1 to 1, as said below
- weights: float32 [8], P('ens'), may hold values from 2 to 8
- target: float32 [512, 512], replicated, may hold values from -1 to 1, as said below
Outputs:
- gradient: float32 [512, 32, 512], P('ens', 'tm')
Inputs may be any that keep to these rules, and one draw needn't show every extreme that they name: Every propagators[m, t] is an orthogonal 512 x 512 matrix up to float32 rounding. target is an orthogonal 512 x 512 matrix up to float32 rounding.
All inputs are finite; a program needn't handle non-finite values.
Results may differ from a plain program's by a relative error of at most 0.0003.
Values sent between devices are 32-bit elements; how exact they have to be, the bound alone decides.
A program may use at most 128 MiB of HBM per device.

v0:
```python
import jax
import jax.numpy as jnp
from jax import lax
from jax.sharding import PartitionSpec as P

highest = lax.Precision.HIGHEST


def carried_in(part, axis, combine, identity):
    place = lax.axis_index(axis)
    gathered = lax.all_gather(part, axis)
    state = jnp.zeros_like(part) + jnp.asarray(identity, part.dtype)

    def one(lap, state):
        return combine(state, lax.dynamic_index_in_dim(gathered, lap, 0, False))

    return lax.fori_loop(0, place, one, state)


def spread(value, axis, root):
    mine = lax.axis_index(axis) == root
    return lax.psum(jnp.where(mine, value, jnp.zeros_like(value)), axis)


def multiply(left_side, right_side):
    return jnp.einsum("mij,mjk->mik", left_side, right_side, precision=highest)


def compose_forward(earlier, later):
    return multiply(later, earlier)


def shards(propagators, weights, target):
    slices = propagators.shape[1]
    order = target.shape[0]
    block_product = propagators[:, 0]
    identity = jnp.broadcast_to(jnp.eye(order, dtype=jnp.float32), block_product.shape)
    before = carried_in(block_product, "tm", compose_forward, identity)
    running = before
    running = multiply(propagators[:, 0], running)
    collected = [running]
    stacked = jnp.stack(collected, axis=1)
    last_prefix = stacked[:, slices - 1]
    final_product = spread(last_prefix, "tm", lax.axis_size("tm") - 1)
    twisted = jnp.einsum("ki,mkj->mij", target, final_product, precision=highest)
    skew_part = weights[:, None, None] * (twisted - jnp.swapaxes(twisted, 1, 2)) * 0.5
    right_factor = jnp.einsum("mij,mtkj->mtik", skew_part, stacked, precision=highest)
    return lax.psum_scatter(
        jnp.einsum("mtik,mtkj->itj", stacked, right_factor, precision=highest),
        "ens",
        scatter_dimension=0,
        tiled=True,
    )


def solution(mesh):
    placed = (P("ens", "tm", None, None), P("ens"), P())
    return jax.shard_map(
        shards, mesh=mesh, in_specs=placed, out_specs=P("ens", "tm", None), check_vma=False
    )
```

profile of v0, /device:TPU:32, one launch (start us, length us, event | category | flops | bytes accessed | tf_op | source)
XLA Modules:
  0.0 446.5 jit_solution(15036979733809586489)
XLA Ops:
  6.5 0.0 copy-start
  6.5 0.0 copy-start.1
  6.5 0.0 all-gather.2.cloned.1.call-start
  6.5 0.7 all-gather.2.cloned.1.call-update
  7.3 0.0 all-reduce.4.cloned.1.call-start
  7.3 0.1 fusion.11
  7.4 123.8 %all-gather.2.cloned.1.call-done = f32[32,1,512,512]{3,2,1,0:T(8,128)} async-done(((f32[1,1,512,512]{3,2,1,0:T(8,128)}), f32[32,1,512,512]{3,2,1,0:T(8,128)}) %all-gather.2.cloned.1.call-update) | async-done | bytes 33554448 | tf_op jit(solution)/shard_map/all_gather | solution.py:11
  131.2 4.7 %fusion.8 = f32[512,512]{1,0:T(8,128)S(1)} fusion(f32[1,1,512,512]{3,2,1,0:T(8,128)} %param.5, f32[1,512,512]{2,1,0:T(8,128)S(1)} %get-tuple-element.28), kind=kOutput, calls=%fused_computation.12 | convolution fusion | flops 1610612736 | bytes 3145728 | tf_op jit(solution)/shard_map/mij,mjk->mik/dot_general | solution.py:26
  135.9 1.1 select_bitcast_fusion
  137.1 0.0 all-reduce.4.cloned.1.call-update
  137.1 0.2 all-reduce.6.cloned.1.call-start
  138.0 211.9 %all-reduce.4.cloned.1.call-done = f32[512,512]{0,1:T(8,128)} async-done(((f32[512,512]{0,1:T(8,128)}), f32[512,512]{0,1:T(8,128)}) %all-reduce.4.cloned.1.call-update) | async-done | bytes 1048592 | tf_op jit(solution)/shard_map/psum | solution.py:22
  349.8 0.0 copy-done
  349.8 3.1 convolution_bitcast_fusion.3
  352.9 1.3 copy.6
  354.2 4.7 %convolution_bitcast_fusion.2 = f32[512,512]{0,1:T(8,128)S(1)} fusion(f32[512,512]{1,0:T(8,128)S(1)} %fusion.8, f32[1,512,512]{2,1,0:T(8,128)S(1)} %convolution_bitcast_fusion.3, f32[1,512,512]{1,2,0:T(8,128)} %copy.6, f32[]{:T(128)} %bitcast.53), kind=kOutput, calls=%fused_computation.6 | convolution fusion | flops 1611399168 | bytes 4194308 | tf_op jit(solution)/shard_map/mij,mtkj->mtik/dot_general | solution.py:47
  358.9 1.8 convolution_bitcast_fusion.1
  360.8 2.0 copy.7
  362.7 0.0 all-reduce.6.cloned.1.call-update
  362.7 0.0 copy-done.1
  362.7 0.6 dynamic-slice
  364.0 74.4 %all-reduce.6.cloned.1.call-done = f32[512,1,512]{2,1,0:T(1,128)} async-done(((f32[512,1,512]{2,1,0:T(1,128)}), f32[512,1,512]{2,1,0:T(1,128)}) %all-reduce.6.cloned.1.call-update) | async-done | bytes 1048592
  438.4 1.6 constant_dynamic-slice_fusion
  (1 shorter events, 0.0 us)
Async XLA Ops:
  6.5 343.3 %copy-start = (f32[512,512]{1,0:T(8,128)S(1)}, f32[512,512]{1,0:T(8,128)}, u32[]{:S(2)}) copy-start(f32[512,512]{1,0:T(8,128)} %param.7) | copy-start | bytes 3145732
  6.5 356.2 %copy-start.1 = (u32[256]{0:T(256)S(1)}, u32[256]{0:T(256)}, u32[]{:S(2)}) copy-start(u32[256]{0:T(256)} %constant.26) | copy-start | bytes 3076
  6.5 124.7 %all-gather.2.cloned.1.call-start = ((), (), s32[]{:S(2)}) async-start(), calls=%async_computation | async-start | bytes 34603008 | tf_op jit(solution)/shard_map/all_gather | solution.py:11
  7.3 342.6 %all-reduce.4.cloned.1.call-start = ((), (), s32[]{:S(2)}) async-start(), calls=%async_computation.1 | async-start | bytes 2097152 | tf_op jit(solution)/shard_map/psum | solution.py:22
  137.1 301.3 %all-reduce.6.cloned.1.call-start = ((), (), s32[]{:S(2)}) async-start(), calls=%async_computation.2 | async-start | bytes 2097152
Sparse Core Ops, SparseCore 0:
  9.9 121.2 all-gather.1
  137.2 212.5 all-reduce.3
  362.9 75.4 all-reduce.5
where the time goes:
time: 449 us; the launch traced here: 446 us
  waiting for transfers between devices  411 us (92%)
  between operations  14.5 us (3%)
  matrix products  14.3 us (3%)
  local copies, waits for them, and re-layouts  5.42 us (1%)
    psum x1, waiting for transfers between devices, spread(): return lax.psum(jnp.where(mine, value, jnp.zeros_like(value)), axis)  212 us
    all_gather x1, waiting for transfers between devices, carried_in(): gathered = lax.all_gather(part, axis)  124 us
    unnamed x4, waiting for transfers between devices  75.1 us
  transfers between devices with their start and end apart: 3, of which 3 were waited for; matrix products, arithmetic and copies ran while one was open for 0% of the time, Pallas kernels for 0%

commit v1 on v0

v1 whole, which is shorter than its diff:
```python
import jax
import jax.numpy as jnp
from jax import lax
from jax.sharding import PartitionSpec as P

highest = lax.Precision.HIGHEST


def shards(propagators, weights, target):
    slot = lax.axis_index("tm")
    slices = lax.axis_size("tm")
    own = propagators[0, 0]
    first = jnp.dot(own, target.T, precision=highest)
    window = jnp.where(slot == 0, first, own)
    step = 1
    while step < slices:
        ring = [(i, (i + step) % slices) for i in range(slices)]
        earlier = lax.ppermute(window, "tm", ring)
        window = jnp.dot(window, earlier, precision=highest)
        step *= 2
    term = (0.5 * weights[0]) * (window - window.T)
    summed = lax.psum_scatter(term, "ens", scatter_dimension=0, tiled=True)
    return summed[:, None, :]


def solution(mesh):
    placed = (P("ens", "tm", None, None), P("ens"), P())
    return jax.shard_map(
        shards, mesh=mesh, in_specs=placed, out_specs=P("ens", "tm", None), check_vma=False
    )
```

time: 449 us -> 181 us (0.40)
  waiting for transfers between devices: 411 us -> 147 us
    psum x1 -> x0, waiting for transfers between devices: 212 us -> none  [spread(): return lax.psum(jnp.where(mine, value, jnp.zeros_like(value)), axis)]
    all_gather x1 -> x0, waiting for transfers between devices: 124 us -> none  [carried_in(): gathered = lax.all_gather(part, axis)]
    ppermute x0 -> x5, waiting for transfers between devices: none -> 105 us  [shards(): earlier = lax.ppermute(window, 'tm', ring)]
    unnamed x4 -> x1, waiting for transfers between devices: 75.1 us -> 0.02 us
    reduce_scatter x0 -> x1, waiting for transfers between devices: none -> 41.7 us  [shards(): summed = lax.psum_scatter(term, 'ens', scatter_dimension=0, tiled=True)]
    dot_general x4 -> x6, matrix products: 14.3 us -> 12.7 us  [the longest x5 9.23 us: shards(): window = jnp.dot(window, earlier, precision=highest)]
  transfers between devices with their start and end apart: 3 -> 6, of which waited for: 3 -> 6; matrix products, arithmetic and copies ran while one was open for 0% -> 0% of each run, Pallas kernels for 0% -> 0%
where the time goes in v1:
time: 181 us; the launch traced here: 180 us
  waiting for transfers between devices  147 us (81%)
  between operations  14.1 us (8%)
  matrix products  12.7 us (7%)
  local copies, waits for them, and re-layouts  3.25 us (2%)
  starting transfers between devices  2.38 us (1%)
    ppermute x5, waiting for transfers between devices, shards(): earlier = lax.ppermute(window, 'tm', ring)  105 us
    reduce_scatter x1, waiting for transfers between devices, shards(): summed = lax.psum_scatter(term, 'ens', scatter_dimension=0, tiled=True)  41.7 us
    dot_general x5, matrix products, shards(): window = jnp.dot(window, earlier, precision=highest)  9.23 us
  transfers between devices with their start and end apart: 6, of which 6 were waited for; matrix products, arithmetic and copies ran while one was open for 0% of the time, Pallas kernels for 0%

profile of v1, /device:TPU:32, one launch (start us, length us, event | category | flops | bytes accessed | tf_op | source)
XLA Modules:
  0.0 180.3 jit_solution(8660192247396520946)
XLA Ops:
  6.5 0.0 copy-start
  6.5 0.0 reduce-scatter.2.cloned.1.call-start
  6.5 1.2 copy-done
  7.8 3.4 %convolution_select_fusion = f32[512,512]{1,0:T(8,128)S(1)} fusion(f32[512,512]{1,0:T(8,128)S(1)} %copy-done, f32[1,1,512,512]{3,2,1,0:T(8,128)} %param.3, pred[]{:T(512)S(6)} %eq.3), kind=kOutput, calls=%fused_computation | convolution fusion | flops 1610874880 | bytes 3145729 | tf_op jit(solution)/shard_map/dot_general | solution.py:13
  11.2 0.1 collective-permute-start
  11.3 17.5 %collective-permute-done = f32[512,512]{1,0:T(8,128)S(1)} collective-permute-done((f32[512,512]{1,0:T(8,128)S(1)}, f32[512,512]{1,0:T(8,128)S(1)}, u32[]{:S(2)}, u32[]{:S(2)}) %collective-permute-start) | collective-permute-done | bytes 1048608 | tf_op jit(solution)/shard_map/ppermute | solution.py:18
  28.8 1.8 %fusion.2 = f32[512,512]{1,0:T(8,128)S(1)} fusion(f32[512,512]{1,0:T(8,128)S(1)} %convolution_select_fusion, f32[512,512]{1,0:T(8,128)S(1)} %collective-permute-done), kind=kOutput, calls=%fused_computation.4 | convolution fusion | flops 1610612736 | bytes 3145728 | tf_op jit(solution)/shard_map/dot_general | solution.py:19
  30.7 0.1 collective-permute-start.1
  30.8 24.3 %collective-permute-done.1 = f32[512,512]{1,0:T(8,128)S(1)} collective-permute-done((f32[512,512]{1,0:T(8,128)S(1)}, f32[512,512]{1,0:T(8,128)S(1)}, u32[]{:S(2)}, u32[]{:S(2)}) %collective-permute-start.1) | collective-permute-done | bytes 1048608 | tf_op jit(solution)/shard_map/ppermute | solution.py:18
  55.0 1.8 %fusion.3 = f32[512,512]{1,0:T(8,128)S(1)} fusion(f32[512,512]{1,0:T(8,128)S(1)} %fusion.2, f32[512,512]{1,0:T(8,128)S(1)} %collective-permute-done.1), kind=kOutput, calls=%fused_computation.5 | convolution fusion | flops 1610612736 | bytes 3145728 | tf_op jit(solution)/shard_map/dot_general | solution.py:19
  56.9 0.1 collective-permute-start.2
  57.0 23.7 %collective-permute-done.2 = f32[512,512]{1,0:T(8,128)S(1)} collective-permute-done((f32[512,512]{1,0:T(8,128)S(1)}, f32[512,512]{1,0:T(8,128)S(1)}, u32[]{:S(2)}, u32[]{:S(2)}) %collective-permute-start.2) | collective-permute-done | bytes 1048608 | tf_op jit(solution)/shard_map/ppermute | solution.py:18
  80.7 1.8 %fusion.4 = f32[512,512]{1,0:T(8,128)S(1)} fusion(f32[512,512]{1,0:T(8,128)S(1)} %fusion.3, f32[512,512]{1,0:T(8,128)S(1)} %collective-permute-done.2), kind=kOutput, calls=%fused_computation.6 | convolution fusion | flops 1610612736 | bytes 3145728 | tf_op jit(solution)/shard_map/dot_general | solution.py:19
  82.5 0.5 collective-permute-start.3
  83.1 20.8 %collective-permute-done.3 = f32[512,512]{1,0:T(8,128)S(1)} collective-permute-done((f32[512,512]{1,0:T(8,128)S(1)}, f32[512,512]{1,0:T(8,128)S(1)}, u32[]{:S(2)}, u32[]{:S(2)}) %collective-permute-start.3) | collective-permute-done | bytes 1048608 | tf_op jit(solution)/shard_map/ppermute | solution.py:18
  103.9 1.8 %fusion.5 = f32[512,512]{1,0:T(8,128)S(1)} fusion(f32[512,512]{1,0:T(8,128)S(1)} %fusion.4, f32[512,512]{1,0:T(8,128)S(1)} %collective-permute-done.3), kind=kOutput, calls=%fused_computation.7 | convolution fusion | flops 1610612736 | bytes 3145728 | tf_op jit(solution)/shard_map/dot_general | solution.py:19
  105.7 1.6 collective-permute-start.4
  108.0 18.7 %collective-permute-done.4 = f32[512,512]{1,0:T(8,128)S(1)} collective-permute-done((f32[512,512]{1,0:T(8,128)S(1)}, f32[512,512]{1,0:T(8,128)S(1)}, u32[]{:S(2)}, u32[]{:S(2)}) %collective-permute-start.4) | collective-permute-done | bytes 1048608 | tf_op jit(solution)/shard_map/ppermute | solution.py:18
  126.7 1.8 %fusion.6 = f32[512,512]{1,0:T(8,128)S(1)} fusion(f32[512,512]{1,0:T(8,128)S(1)} %fusion.5, f32[512,512]{1,0:T(8,128)S(1)} %collective-permute-done.4), kind=kOutput, calls=%fused_computation.8 | convolution fusion | flops 1610612736 | bytes 3145728 | tf_op jit(solution)/shard_map/dot_general | solution.py:19
  128.5 0.3 copy.4
  128.9 1.2 fusion
  130.1 0.0 reduce-scatter.2.cloned.1.call-update
  130.1 41.7 %reduce-scatter.2.cloned.1.call-done = f32[64,512]{1,0:T(8,128)} async-done(((f32[512,512]{1,0:T(8,128)}), f32[64,512]{1,0:T(8,128)}) %reduce-scatter.2.cloned.1.call-update) | async-done | bytes 131088 | tf_op jit(solution)/shard_map/reduce_scatter | solution.py:22
  171.8 1.7 copy.5
Async XLA Ops:
  6.5 1.2 copy-start
  6.5 165.2 %reduce-scatter.2.cloned.1.call-start = ((), (), s32[]{:S(2)}) async-start(), calls=%async_computation.1 | async-start | bytes 1179648 | tf_op jit(solution)/shard_map/reduce_scatter | solution.py:22
  11.2 17.6 %collective-permute-start = (f32[512,512]{1,0:T(8,128)S(1)}, f32[512,512]{1,0:T(8,128)S(1)}, u32[]{:S(2)}, u32[]{:S(2)}) collective-permute-start(f32[512,512]{1,0:T(8,128)S(1)} %convolution_select_fusion), channel_id=1, source_target_pairs={{0,8},{8,16},{16,24},{24,32},{32,40},{40,48},{48,56},{56,64},{64,7... | collective-permute-start | bytes 3145736 | tf_op jit(solution)/shard_map/ppermute | solution.py:18
  30.7 24.4 %collective-permute-start.1 = (f32[512,512]{1,0:T(8,128)S(1)}, f32[512,512]{1,0:T(8,128)S(1)}, u32[]{:S(2)}, u32[]{:S(2)}) collective-permute-start(f32[512,512]{1,0:T(8,128)S(1)} %fusion.2), channel_id=1, source_target_pairs={{0,16},{8,24},{16,32},{24,40},{32,48},{40,56},{48,64},{56,72},{64,... | collective-permute-start | bytes 3145736 | tf_op jit(solution)/shard_map/ppermute | solution.py:18
  56.9 23.8 %collective-permute-start.2 = (f32[512,512]{1,0:T(8,128)S(1)}, f32[512,512]{1,0:T(8,128)S(1)}, u32[]{:S(2)}, u32[]{:S(2)}) collective-permute-start(f32[512,512]{1,0:T(8,128)S(1)} %fusion.3), channel_id=1, source_target_pairs={{0,32},{8,40},{16,48},{24,56},{32,64},{40,72},{48,80},{56,88},{64,... | collective-permute-start | bytes 3145736 | tf_op jit(solution)/shard_map/ppermute | solution.py:18
  82.5 21.3 %collective-permute-start.3 = (f32[512,512]{1,0:T(8,128)S(1)}, f32[512,512]{1,0:T(8,128)S(1)}, u32[]{:S(2)}, u32[]{:S(2)}) collective-permute-start(f32[512,512]{1,0:T(8,128)S(1)} %fusion.4), channel_id=1, source_target_pairs={{0,64},{8,72},{16,80},{24,88},{32,96},{40,104},{48,112},{56,120},{... | collective-permute-start | bytes 3145736 | tf_op jit(solution)/shard_map/ppermute | solution.py:18
  105.7 21.0 %collective-permute-start.4 = (f32[512,512]{1,0:T(8,128)S(1)}, f32[512,512]{1,0:T(8,128)S(1)}, u32[]{:S(2)}, u32[]{:S(2)}) collective-permute-start(f32[512,512]{1,0:T(8,128)S(1)} %fusion.5), channel_id=1, source_target_pairs={{0,128},{8,136},{16,144},{24,152},{32,160},{40,168},{48,176},{56,1... | collective-permute-start | bytes 3145736 | tf_op jit(solution)/shard_map/ppermute | solution.py:18
Sparse Core Ops, SparseCore 0:
  130.2 41.4 reduce-scatter.1

commit v2 on v1

v2 whole, which is shorter than its diff:
```python
import functools

import jax
import jax.numpy as jnp
from jax import lax
from jax.experimental import pallas as pl
from jax.experimental.pallas import tpu as pltpu
from jax.sharding import PartitionSpec as P

MESH = pl.DeviceIdType.MESH
R = 512
HALF = R // 2
PIECE = 128
SMALL = 64
ROWS = 64
CHUNK = 16
COPIES = 96


def split(value):
    high = value.astype(jnp.bfloat16)
    low = (value - high.astype(jnp.float32)).astype(jnp.bfloat16)
    return high, low


def kernel(
    prop_ref, target_ref, weight_ref, out_ref,
    pair, target, chips, halves, rows, left, right, va, vb, mid, grad,
    long_in, short_in, bh, bl, send_sem, recv_sem, local_sem,
):
    slot = lax.axis_index("tm")
    z = lax.axis_index("ens")
    core = lax.rem(slot, 2)
    y = lax.rem(slot // 2, 4)
    x = slot // 8

    def at(x_, y_, core_):
        return ((x_ * 4 + y_) * 2 + core_, z)

    xp, xm, xo = lax.rem(x + 1, 4), lax.rem(x + 3, 4), lax.rem(x + 2, 4)
    yp, ym, yo = lax.rem(y + 1, 4), lax.rem(y + 3, 4), lax.rem(y + 2, 4)
    sibling = at(x, y, 1 - core)
    to_yp, to_ym = at(x, yp, core), at(x, ym, core)
    to_xp, to_xm = at(xp, y, core), at(xm, y, core)
    to_long = (slot, lax.rem(z + 1 + 6 * core, 8))
    to_short = (slot, lax.rem(z + 7 - 6 * core, 8))

    own_load = pltpu.make_async_copy(prop_ref, pair.at[core], local_sem.at[0])
    own_load.start()
    target_load = pltpu.make_async_copy(target_ref, target, local_sem.at[1])
    target_load.start()

    barrier = pltpu.get_barrier_semaphore()
    peers = (sibling, to_yp, to_ym, to_xp, to_xm, to_long, to_short)
    for peer in peers:
        pl.semaphore_signal(barrier, inc=1, device_id=peer, device_id_type=MESH)
    pl.semaphore_wait(barrier, len(peers))

    started = []

    def send(src, dst, device):
        n = len(started)
        copy = pltpu.make_async_remote_copy(
            src_ref=src, dst_ref=dst, send_sem=send_sem.at[n], recv_sem=recv_sem.at[n],
            device_id=device, device_id_type=MESH,
        )
        copy.start()
        started.append(copy)
        return copy

    def prepare(b):
        high, low = split(b[...])
        bh[...] = high
        bl[...] = low

    def product_rows(dst, a, start, count, nt=False):
        dims = (((1,), (1 if nt else 0,)), ((), ()))

        def dot(p, q):
            return lax.dot_general(p, q, dims, preferred_element_type=jnp.float32)

        block = pl.ds(start, count)
        high, low = split(a[block, :])
        dst[block, :] = dot(high, bh[...]) + (dot(high, bl[...]) + dot(low, bh[...]))

    def product(dst, a, b, nt=False):
        prepare(b)

        def one(i, _):
            product_rows(dst, a, pl.multiple_of(i * HALF, HALF), HALF, nt)
            return 0

        lax.fori_loop(0, 2, one, 0)

    swap = send(prop_ref, pair.at[core], sibling)
    own_load.wait()
    target_load.wait()
    swap.wait_recv()

    @pl.when(slot // 2 == 0)
    def _():
        product(pair.at[0], pair.at[0], target, nt=True)

    mine = pl.multiple_of(core * HALF, HALF)
    other = pl.multiple_of((1 - core) * HALF, HALF)
    first, second = pl.ds(mine, PIECE), pl.ds(mine + PIECE, PIECE)
    prepare(pair.at[0])
    own = chips.at[y]
    product_rows(own, pair.at[1], mine, PIECE)
    up0 = send(own.at[first], own.at[first], to_yp)
    product_rows(own, pair.at[1], pl.multiple_of(mine + PIECE, PIECE), PIECE)
    down0 = send(own.at[second], own.at[second], to_ym)
    up1 = send(own.at[second], own.at[second], to_yp)
    down1 = send(own.at[first], own.at[first], to_ym)
    product_rows(own, pair.at[1], other, HALF)

    def pass_on(ref, block):
        return send(ref.at[block], ref.at[block], sibling)

    up0.wait_recv()
    up2 = send(chips.at[ym].at[first], chips.at[ym].at[first], to_yp)
    near = [pass_on(chips.at[ym], first)]
    down0.wait_recv()
    down2 = send(chips.at[yp].at[second], chips.at[yp].at[second], to_ym)
    near.append(pass_on(chips.at[yp], second))
    up1.wait_recv()
    near.append(pass_on(chips.at[ym], second))
    down1.wait_recv()
    near.append(pass_on(chips.at[yp], first))
    for copy in near:
        copy.wait_recv()
    here = y // 2
    product(halves.at[here], chips.at[2 * here + 1], chips.at[2 * here])
    up2.wait_recv()
    far = [pass_on(chips.at[yo], first)]
    down2.wait_recv()
    far.append(pass_on(chips.at[yo], second))
    for copy in far:
        copy.wait_recv()
    product(halves.at[1 - here], chips.at[3 - 2 * here], chips.at[2 - 2 * here])

    half = lax.rem(y, 2)

    def piece(half_, number):
        return pl.ds(pl.multiple_of(half_ * HALF + number * SMALL, SMALL), SMALL)

    a_here, b_here = piece(half, core), piece(half, 2 + core)
    a_there, b_there = piece(1 - half, core), piece(1 - half, 2 + core)
    prepare(halves.at[0])
    row = rows.at[x]
    product_rows(row, halves.at[1], pl.multiple_of(half * HALF, HALF), HALF)
    xu_a = send(row.at[a_here], row.at[a_here], to_xp)
    xd_b = send(row.at[b_here], row.at[b_here], to_xm)
    xu_b = send(row.at[b_here], row.at[b_here], to_xp)
    xd_a = send(row.at[a_here], row.at[a_here], to_xm)
    product_rows(row, halves.at[1], pl.multiple_of((1 - half) * HALF, HALF), HALF)

    def take(copy, ref, block, onward):
        copy.wait_recv()
        return send(ref.at[block], ref.at[block], onward), pass_on(ref, block)

    xu_a.wait_recv()
    xu_r = send(rows.at[xm].at[a_here], rows.at[xm].at[a_here], to_xp)
    y1 = send(rows.at[xm].at[a_here], rows.at[xm].at[a_here], to_yp)
    by_sibling = [pass_on(rows.at[xm], a_here)]
    xd_b.wait_recv()
    xd_r = send(rows.at[xp].at[b_here], rows.at[xp].at[b_here], to_xm)
    y2 = send(rows.at[xp].at[b_here], rows.at[xp].at[b_here], to_ym)
    by_sibling.append(pass_on(rows.at[xp], b_here))
    y3, got = take(xu_b, rows.at[xm], b_here, to_ym)
    by_sibling.append(got)
    y4, got = take(xd_a, rows.at[xp], a_here, to_yp)
    by_sibling.append(got)

    left[...] = jnp.where(core == 0, pair[0], own[...])

    def extend(i, _):
        product(left, left, chips.at[y - 1 - i])
        return 0

    lax.fori_loop(0, y, extend, 0)
    product(right, row, left, nt=True)

    y5, got = take(xu_r, rows.at[xo], a_here, to_yp)
    last_sibling = [got]
    y6, got = take(xd_r, rows.at[xo], b_here, to_ym)
    last_sibling.append(got)
    for copy, at_row, block in (
        (y1, xm, a_there), (y2, xp, b_there), (y3, xm, b_there), (y4, xp, a_there),
    ):
        copy.wait_recv()
        by_sibling.append(pass_on(rows.at[at_row], block))
    for copy in by_sibling:
        copy.wait_recv()
    product(va, left, rows.at[xm])
    product(vb, rows.at[xp], right)
    for copy, block in ((y5, a_there), (y6, b_there)):
        copy.wait_recv()
        last_sibling.append(pass_on(rows.at[xo], block))
    for copy in last_sibling:
        copy.wait_recv()
    product(mid, rows.at[xo], vb)
    product(right, va, mid)
    scale = 0.5 * weight_ref[0]
    turned = right[...]
    grad[...] = scale * (turned - turned.T)

    chunks = ROWS // CHUNK

    def own_rows(owner, q):
        return pl.ds(pl.multiple_of(owner * ROWS + q * CHUNK, CHUNK), CHUNK)

    def owner_long(step):
        return lax.rem(z + (4 - step) + core * 2 * (4 + step), 8)

    def owner_short(step):
        return lax.rem(z + 5 + step + core * 2 * (3 - step), 8)

    long_copies, short_copies = [], []
    for step in range(4):
        for q in range(chunks):
            spot = pl.ds(q * CHUNK, CHUNK)
            block = own_rows(owner_long(step), q)
            if step == 0:
                src = grad.at[block]
            else:
                long_copies[(step - 1) * chunks + q].wait_recv()
                src = long_in.at[step - 1].at[spot]
                src[...] += grad[block, :]
            long_copies.append(send(src, long_in.at[step].at[spot], to_long))
            if step == 3:
                continue
            block = own_rows(owner_short(step), q)
            if step == 0:
                src = grad.at[block]
            else:
                short_copies[(step - 1) * chunks + q].wait_recv()
                src = short_in.at[step - 1].at[spot]
                src[...] += grad[block, :]
            short_copies.append(send(src, short_in.at[step].at[spot], to_short))
    for q in range(chunks):
        spot = pl.ds(q * CHUNK, CHUNK)
        short_copies[2 * chunks + q].wait_recv()
        long_copies[3 * chunks + q].wait_recv()
        out_ref[spot, :] = (
            grad[own_rows(z, q), :] + long_in[3, spot, :] + short_in[2, spot, :]
        )
    for copy in started:
        copy.wait_send()
    assert len(started) <= COPIES


def shards(propagators, weights, target):
    full = pltpu.VMEM((R, R), jnp.float32)
    summed = pl.pallas_call(
        kernel,
        out_shape=jax.ShapeDtypeStruct((ROWS, R), jnp.float32),
        in_specs=[
            pl.BlockSpec(memory_space=pl.ANY),
            pl.BlockSpec(memory_space=pl.ANY),
            pl.BlockSpec(memory_space=pltpu.SMEM),
        ],
        out_specs=pl.BlockSpec(memory_space=pltpu.VMEM),
        scratch_shapes=[
            pltpu.VMEM((2, R, R), jnp.float32),
            full,
            pltpu.VMEM((4, R, R), jnp.float32),
            pltpu.VMEM((2, R, R), jnp.float32),
            pltpu.VMEM((4, R, R), jnp.float32),
            full, full, full, full, full, full,
            pltpu.VMEM((4, ROWS, R), jnp.float32),
            pltpu.VMEM((3, ROWS, R), jnp.float32),
            pltpu.VMEM((R, R), jnp.bfloat16),
            pltpu.VMEM((R, R), jnp.bfloat16),
            pltpu.SemaphoreType.DMA((COPIES,)),
            pltpu.SemaphoreType.DMA((COPIES,)),
            pltpu.SemaphoreType.DMA((2,)),
        ],
        compiler_params=pltpu.CompilerParams(
            collective_id=0, has_side_effects=True, vmem_limit_bytes=56 * 1024 * 1024
        ),
        name="grape",
    )(propagators[0, 0], target, weights)
    return summed[:, None, :]


def solution(mesh):
    placed = (P("ens", "tm", None, None), P("ens"), P())
    return jax.shard_map(
        shards, mesh=mesh, in_specs=placed, out_specs=P("ens", "tm", None), check_vma=False
    )
```

time: 181 us -> 76.1 us (0.42)
  waiting for transfers between devices: 147 us -> 0 us
  Pallas kernels: 0 us -> 72.8 us
  between operations: 14.1 us -> 0.66 us
  matrix products: 12.7 us -> 0 us
  starting transfers between devices: 2.38 us -> 0 us
    ppermute x5 -> x0, waiting for transfers between devices: 105 us -> none  [shards(): earlier = lax.ppermute(window, 'tm', ring)]
    pallas_call x0 -> x1, Pallas kernels: none -> 72.8 us  [shards(): pl.pallas_call(kernel, out_shape=jax.ShapeDtypeStruct((ROWS, R), jnp.floa...]
    reduce_scatter x1 -> x0, waiting for transfers between devices: 41.7 us -> none  [shards(): summed = lax.psum_scatter(term, 'ens', scatter_dimension=0, tiled=True)]
    dot_general x6 -> x0, matrix products: 12.7 us -> none  [the longest x5 9.23 us: shards(): window = jnp.dot(window, earlier, precision=highest)]
    ppermute x5 -> x0, starting transfers between devices: 2.37 us -> none  [shards(): earlier = lax.ppermute(window, 'tm', ring)]
  transfers between devices with their start and end apart: 6 -> 0, of which waited for: 6 -> 0; matrix products, arithmetic and copies ran while one was open for 0% -> 0% of each run, Pallas kernels for 0% -> 0%
where the time goes in v2:
time: 76.1 us; the launch traced here: 75.1 us
  Pallas kernels  72.8 us (96%)
  local copies, waits for them, and re-layouts  1.69 us (2%)
    pallas_call x1, Pallas kernels, shards(): pl.pallas_call(kernel, out_shape=jax.ShapeDtypeStruct((ROWS, R), jnp.floa...  72.8 us
    broadcast_in_dim x1, local copies, waits for them, and re-layouts, shards(): return summed[:, None, :]  1.69 us

profile of v2, /device:TPU:32, one launch (start us, length us, event | category | flops | bytes accessed | tf_op | source)
XLA Modules:
  0.0 75.1 jit_solution(2813318396698052550)
XLA Ops:
  0.7 72.8 %grape.1 = f32[64,512]{1,0:T(8,128)} custom-call(f32[512,512]{1,0:T(8,128)} %bitcast.2, f32[512,512]{1,0:T(8,128)} %target_ref.1, f32[1]{0:T(128)S(6)} %copy.5.weight_ref), custom_call_target="tpu_custom_call" | custom-call | tf_op jit(solution)/shard_map/grape/pallas_call | solution.py:255
  73.4 1.7 %copy.4 = f32[64,1,512]{2,1,0:T(1,128)} copy(f32[64,1,512]{2,0,1:T(8,128)} %bitcast.3) | data formatting | bytes 262144 | tf_op jit(solution)/shard_map/broadcast_in_dim | solution.py:284

commit v3 on v2

--- a/solution.py
+++ b/solution.py
@@ -12,9 +12,10 @@
 HALF = R // 2
 PIECE = 128
 SMALL = 64
+SUB = 32
 ROWS = 64
 CHUNK = 16
-COPIES = 96
+COPIES = 160
 
 
 def split(value):
@@ -25,7 +26,7 @@
 
 def kernel(
     prop_ref, target_ref, weight_ref, out_ref,
-    pair, target, chips, halves, rows, left, right, va, vb, mid, grad,
+    ends, target, mats, rows, strip, va, vb, mid, full, grad,
     long_in, short_in, bh, bl, send_sem, recv_sem, local_sem,
 ):
     slot = lax.axis_index("tm")
@@ -45,7 +46,7 @@
     to_long = (slot, lax.rem(z + 1 + 6 * core, 8))
     to_short = (slot, lax.rem(z + 7 - 6 * core, 8))
 
-    own_load = pltpu.make_async_copy(prop_ref, pair.at[core], local_sem.at[0])
+    own_load = pltpu.make_async_copy(prop_ref, ends.at[core], local_sem.at[0])
     own_load.start()
     target_load = pltpu.make_async_copy(target_ref, target, local_sem.at[1])
     target_load.start()
@@ -92,117 +93,191 @@
 
         lax.fori_loop(0, 2, one, 0)
 
-    swap = send(prop_ref, pair.at[core], sibling)
+    swap = send(prop_ref, ends.at[core], sibling)
     own_load.wait()
-    target_load.wait()
     swap.wait_recv()
-
-    @pl.when(slot // 2 == 0)
-    def _():
-        product(pair.at[0], pair.at[0], target, nt=True)
-
     mine = pl.multiple_of(core * HALF, HALF)
     other = pl.multiple_of((1 - core) * HALF, HALF)
     first, second = pl.ds(mine, PIECE), pl.ds(mine + PIECE, PIECE)
-    prepare(pair.at[0])
-    own = chips.at[y]
-    product_rows(own, pair.at[1], mine, PIECE)
+    prepare(ends.at[0])
+    own = mats.at[y]
+    product_rows(own, ends.at[1], mine, PIECE)
     up0 = send(own.at[first], own.at[first], to_yp)
-    product_rows(own, pair.at[1], pl.multiple_of(mine + PIECE, PIECE), PIECE)
+    product_rows(own, ends.at[1], pl.multiple_of(mine + PIECE, PIECE), PIECE)
     down0 = send(own.at[second], own.at[second], to_ym)
     up1 = send(own.at[second], own.at[second], to_yp)
     down1 = send(own.at[first], own.at[first], to_ym)
-    product_rows(own, pair.at[1], other, HALF)
+    product_rows(own, ends.at[1], other, HALF)
+
+    @pl.when(core == 1)
+    def _():
+        ends[0] = own[...]
+        down = lax.broadcasted_iota(jnp.int32, (R, R), 0)
+        across = lax.broadcasted_iota(jnp.int32, (R, R), 1)
+        ends[1] = jnp.where(down == across, 1.0, 0.0).astype(jnp.float32)
 
     def pass_on(ref, block):
         return send(ref.at[block], ref.at[block], sibling)
 
     up0.wait_recv()
-    up2 = send(chips.at[ym].at[first], chips.at[ym].at[first], to_yp)
-    near = [pass_on(chips.at[ym], first)]
+    up2 = send(mats.at[ym].at[first], mats.at[ym].at[first], to_yp)
+    near = [pass_on(mats.at[ym], first)]
     down0.wait_recv()
-    down2 = send(chips.at[yp].at[second], chips.at[yp].at[second], to_ym)
-    near.append(pass_on(chips.at[yp], second))
+    down2 = send(mats.at[yp].at[second], mats.at[yp].at[second], to_ym)
+    near.append(pass_on(mats.at[yp], second))
     up1.wait_recv()
-    near.append(pass_on(chips.at[ym], second))
+    near.append(pass_on(mats.at[ym], second))
     down1.wait_recv()
-    near.append(pass_on(chips.at[yp], first))
+    near.append(pass_on(mats.at[yp], first))
     for copy in near:
         copy.wait_recv()
-    here = y // 2
-    product(halves.at[here], chips.at[2 * here + 1], chips.at[2 * here])
+    late, odd = y // 2, lax.rem(y, 2)
+    product(mats.at[4 + late], mats.at[2 * late + 1], mats.at[2 * late])
+
+    @pl.when(odd == 0)
+    def _():
+        product(ends.at[2], mats.at[2 * late + 1], ends.at[1])
+
+    @pl.when(odd == 1)
+    def _():
+        product(ends.at[2], ends.at[0], mats.at[2 * late])
+
     up2.wait_recv()
-    far = [pass_on(chips.at[yo], first)]
+    far = [pass_on(mats.at[yo], first)]
     down2.wait_recv()
-    far.append(pass_on(chips.at[yo], second))
+    far.append(pass_on(mats.at[yo], second))
     for copy in far:
         copy.wait_recv()
-    product(halves.at[1 - here], chips.at[3 - 2 * here], chips.at[2 - 2 * here])
-
-    half = lax.rem(y, 2)
-
-    def piece(half_, number):
-        return pl.ds(pl.multiple_of(half_ * HALF + number * SMALL, SMALL), SMALL)
-
-    a_here, b_here = piece(half, core), piece(half, 2 + core)
-    a_there, b_there = piece(1 - half, core), piece(1 - half, 2 + core)
-    prepare(halves.at[0])
-    row = rows.at[x]
-    product_rows(row, halves.at[1], pl.multiple_of(half * HALF, HALF), HALF)
-    xu_a = send(row.at[a_here], row.at[a_here], to_xp)
-    xd_b = send(row.at[b_here], row.at[b_here], to_xm)
-    xu_b = send(row.at[b_here], row.at[b_here], to_xp)
-    xd_a = send(row.at[a_here], row.at[a_here], to_xm)
-    product_rows(row, halves.at[1], pl.multiple_of((1 - half) * HALF, HALF), HALF)
-
-    def take(copy, ref, block, onward):
-        copy.wait_recv()
-        return send(ref.at[block], ref.at[block], onward), pass_on(ref, block)
-
-    xu_a.wait_recv()
-    xu_r = send(rows.at[xm].at[a_here], rows.at[xm].at[a_here], to_xp)
-    y1 = send(rows.at[xm].at[a_here], rows.at[xm].at[a_here], to_yp)
-    by_sibling = [pass_on(rows.at[xm], a_here)]
-    xd_b.wait_recv()
-    xd_r = send(rows.at[xp].at[b_here], rows.at[xp].at[b_here], to_xm)
-    y2 = send(rows.at[xp].at[b_here], rows.at[xp].at[b_here], to_ym)
-    by_sibling.append(pass_on(rows.at[xp], b_here))
-    y3, got = take(xu_b, rows.at[xm], b_here, to_ym)
-    by_sibling.append(got)
-    y4, got = take(xd_a, rows.at[xp], a_here, to_yp)
-    by_sibling.append(got)
-
-    left[...] = jnp.where(core == 0, pair[0], own[...])
-
-    def extend(i, _):
-        product(left, left, chips.at[y - 1 - i])
-        return 0
-
-    lax.fori_loop(0, y, extend, 0)
-    product(right, row, left, nt=True)
-
-    y5, got = take(xu_r, rows.at[xo], a_here, to_yp)
-    last_sibling = [got]
-    y6, got = take(xd_r, rows.at[xo], b_here, to_ym)
-    last_sibling.append(got)
-    for copy, at_row, block in (
-        (y1, xm, a_there), (y2, xp, b_there), (y3, xm, b_there), (y4, xp, a_there),
-    ):
-        copy.wait_recv()
-        by_sibling.append(pass_on(rows.at[at_row], block))
-    for copy in by_sibling:
-        copy.wait_recv()
-    product(va, left, rows.at[xm])
-    product(vb, rows.at[xp], right)
-    for copy, block in ((y5, a_there), (y6, b_there)):
-        copy.wait_recv()
-        last_sibling.append(pass_on(rows.at[xo], block))
-    for copy in last_sibling:
-        copy.wait_recv()
-    product(mid, rows.at[xo], vb)
-    product(right, va, mid)
+
+    subs = SMALL // SUB
+
+    def pieces(half, number):
+        start = half * HALF + number * SMALL
+        return [pl.ds(pl.multiple_of(start + n * SUB, SUB), SUB) for n in range(subs)]
+
+    a_here, b_here = pieces(odd, core), pieces(odd, 2 + core)
+    a_there, b_there = pieces(1 - odd, core), pieces(1 - odd, 2 + core)
+    begin = mats.at[3 + 2 * late]
+    for n in range(subs):
+        strip[n * SUB:(n + 1) * SUB, :] = begin[a_here[n], :]
+        strip[SMALL + n * SUB:SMALL + (n + 1) * SUB, :] = begin[b_here[n], :]
+    prepare(mats.at[2 - late])
+    product_rows(strip, strip, 0, 2 * SMALL)
+    prepare(mats.at[4 - 4 * late])
+    product_rows(strip, strip, 0, 2 * SMALL)
+    target_load.wait()
+
+    @pl.when(x == 0)
+    def _():
+        prepare(target)
+        product_rows(strip, strip, 0, 2 * SMALL, nt=True)
+
+    strip_a = [strip.at[pl.ds(n * SUB, SUB)] for n in range(subs)]
+    strip_b = [strip.at[pl.ds(SMALL + n * SUB, SUB)] for n in range(subs)]
+    own_row = rows.at[x]
+    xu_a, xd_b, xu_b, xd_a = [], [], [], []
+    for n in range(subs):
+        xu_a.append(send(strip_a[n], own_row.at[a_here[n]], to_xp))
+        xd_b.append(send(strip_b[n], own_row.at[b_here[n]], to_xm))
+    for n in range(subs):
+        xu_b.append(send(strip_b[n], own_row.at[b_here[n]], to_xp))
+        xd_a.append(send(strip_a[n], own_row.at[a_here[n]], to_xm))
+
+    product(mats.at[5 - late], mats.at[3 - 2 * late], mats.at[2 - 2 * late])
+
+    @pl.when(late == 0)
+    def _():
+        product(ends.at[3], mats.at[5], ends.at[2 - odd])
+
+    @pl.when(late == 1)
+    def _():
+        product(ends.at[3], ends.at[2 * odd], mats.at[4])
+
+    left = ends.at[(1 - late) * 2 * odd + late * 3]
+    right = ends.at[(1 - late) * 3 + late * (2 - odd)]
+
+    close_x, close_y, far_x, far_y = [], [], [], []
+    onward, relays_u, relays_d = [], [], []
+
+    def forward(copy, at_row, block, to_y, relay=None):
+        copy.wait_recv()
+        part = rows.at[at_row].at[block]
+        relayed = None if relay is None else send(part, part, relay)
+        return relayed, send(part, part, to_y), send(part, part, sibling)
+
+    for n in range(subs):
+        relayed, up, got = forward(xu_a[n], xm, a_here[n], to_yp, to_xp)
+        relays_u.append(relayed)
+        onward.append((up, xm, a_there[n]))
+        close_x.append(got)
+        relayed, up, got = forward(xd_b[n], xp, b_here[n], to_ym, to_xm)
+        relays_d.append(relayed)
+        onward.append((up, xp, b_there[n]))
+        close_x.append(got)
+    for n in range(subs):
+        _, up, got = forward(xu_b[n], xm, b_here[n], to_ym)
+        onward.append((up, xm, b_there[n]))
+        close_x.append(got)
+        _, up, got = forward(xd_a[n], xp, a_here[n], to_yp)
+        onward.append((up, xp, a_there[n]))
+        close_x.append(got)
+    onward_far = []
+    for n in range(subs):
+        _, up, got = forward(relays_u[n], xo, a_here[n], to_yp)
+        onward_far.append((up, a_there[n]))
+        far_x.append(got)
+        _, up, got = forward(relays_d[n], xo, b_here[n], to_ym)
+        onward_far.append((up, b_there[n]))
+        far_x.append(got)
+
+    @pl.when(x == 0)
+    def _():
+        product(left, left, target, nt=True)
+
+    def pass_some(some):
+        for copy, at_row, block in some:
+            copy.wait_recv()
+            close_y.append(pass_on(rows.at[at_row], block))
+
+    near_half = pl.multiple_of(odd * HALF, HALF)
+    far_half = pl.multiple_of((1 - odd) * HALF, HALF)
+
+    def add_half(dst, a, b, start, first):
+        block = pl.ds(start, HALF)
+        b_high, b_low = split(b[block, :])
+        high, low = split(a[:, block])
+
+        def dot(p, q):
+            return jnp.dot(p, q, preferred_element_type=jnp.float32)
+
+        value = dot(high, b_high) + (dot(high, b_low) + dot(low, b_high))
+        dst[...] = value if first else dst[...] + value
+
+    pass_some(onward[:2 * subs])
+    for copy in close_x:
+        copy.wait_recv()
+    add_half(va, left, rows.at[xm], near_half, True)
+    prepare(right)
+    product_rows(vb, rows.at[xp], near_half, HALF)
+    pass_some(onward[2 * subs:])
+    for copy in close_y:
+        copy.wait_recv()
+    add_half(va, left, rows.at[xm], far_half, False)
+    product_rows(vb, rows.at[xp], far_half, HALF)
+    for copy, block in onward_far:
+        copy.wait_recv()
+        far_y.append(pass_on(rows.at[xo], block))
+    for copy in far_x:
+        copy.wait_recv()
+    prepare(vb)
+    product_rows(mid, rows.at[xo], near_half, HALF)
+    add_half(full, va, mid, near_half, True)
+    for copy in far_y:
+        copy.wait_recv()
+    product_rows(mid, rows.at[xo], far_half, HALF)
+    add_half(full, va, mid, far_half, False)
     scale = 0.5 * weight_ref[0]
-    turned = right[...]
+    turned = full[...]
     grad[...] = scale * (turned - turned.T)
 
     chunks = ROWS // CHUNK
@@ -262,12 +337,12 @@
         ],
         out_specs=pl.BlockSpec(memory_space=pltpu.VMEM),
         scratch_shapes=[
-            pltpu.VMEM((2, R, R), jnp.float32),
+            pltpu.VMEM((4, R, R), jnp.float32),
             full,
+            pltpu.VMEM((6, R, R), jnp.float32),
             pltpu.VMEM((4, R, R), jnp.float32),
-            pltpu.VMEM((2, R, R), jnp.float32),
-            pltpu.VMEM((4, R, R), jnp.float32),
-            full, full, full, full, full, full,
+            pltpu.VMEM((2 * SMALL, R), jnp.float32),
+            full, full, full, full, full,
             pltpu.VMEM((4, ROWS, R), jnp.float32),
             pltpu.VMEM((3, ROWS, R), jnp.float32),
             pltpu.VMEM((R, R), jnp.bfloat16),

time: 76.1 us -> 71.8 us (0.943); the launches traced: 75.1 us -> 71.7 us
  Pallas kernels: 72.8 us -> 69.4 us
    pallas_call x1, Pallas kernels: 72.8 us -> 69.4 us  [shards(): pl.pallas_call(kernel, out_shape=jax.ShapeDtypeStruct((ROWS, R), jnp.floa...]
where the time goes in v3:
time: 71.8 us; the launch traced here: 71.7 us
  Pallas kernels  69.4 us (97%)
  local copies, waits for them, and re-layouts  1.69 us (2%)
    pallas_call x1, Pallas kernels, shards(): pl.pallas_call(kernel, out_shape=jax.ShapeDtypeStruct((ROWS, R), jnp.floa...  69.4 us
    broadcast_in_dim x1, local copies, waits for them, and re-layouts, shards(): return summed[:, None, :]  1.69 us

profile of v3, /device:TPU:32, one launch (start us, length us, event | category | flops | bytes accessed | tf_op | source)
XLA Modules:
  0.0 71.7 jit_solution(11372544744038994947)
XLA Ops:
  0.7 69.4 %grape.1 = f32[64,512]{1,0:T(8,128)} custom-call(f32[512,512]{1,0:T(8,128)} %bitcast.2, f32[512,512]{1,0:T(8,128)} %target_ref.1, f32[1]{0:T(128)S(6)} %copy.5.weight_ref), custom_call_target="tpu_custom_call" | custom-call | tf_op jit(solution)/shard_map/grape/pallas_call | solution.py:330
  70.0 1.7 %copy.4 = f32[64,1,512]{2,1,0:T(1,128)} copy(f32[64,1,512]{2,0,1:T(8,128)} %bitcast.3) | data formatting | bytes 262144 | tf_op jit(solution)/shard_map/broadcast_in_dim | solution.py:359

commit v4 on v3

--- a/solution.py
+++ b/solution.py
@@ -291,28 +291,24 @@
     def owner_short(step):
         return lax.rem(z + 5 + step + core * 2 * (3 - step), 8)
 
+    def hop(copies, step, q, owner, landed, device):
+        spot = pl.ds(q * CHUNK, CHUNK)
+        block = own_rows(owner(step), q)
+        if step == 0:
+            src = grad.at[block]
+        else:
+            copies[(step - 1) * chunks + q].wait_recv()
+            src = landed.at[step - 1].at[spot]
+            src[...] += grad[block, :]
+        copies.append(send(src, landed.at[step].at[spot], device))
+
     long_copies, short_copies = [], []
     for step in range(4):
         for q in range(chunks):
-            spot = pl.ds(q * CHUNK, CHUNK)
-            block = own_rows(owner_long(step), q)
-            if step == 0:
-                src = grad.at[block]
-            else:
-                long_copies[(step - 1) * chunks + q].wait_recv()
-                src = long_in.at[step - 1].at[spot]
-                src[...] += grad[block, :]
-            long_copies.append(send(src, long_in.at[step].at[spot], to_long))
-            if step == 3:
-                continue
-            block = own_rows(owner_short(step), q)
-            if step == 0:
-                src = grad.at[block]
-            else:
-                short_copies[(step - 1) * chunks + q].wait_recv()
-                src = short_in.at[step - 1].at[spot]
-                src[...] += grad[block, :]
-            short_copies.append(send(src, short_in.at[step].at[spot], to_short))
+            hop(long_copies, step, q, owner_long, long_in, to_long)
+        if step < 3:
+            for q in range(chunks):
+                hop(short_copies, step, q, owner_short, short_in, to_short)
     for q in range(chunks):
         spot = pl.ds(q * CHUNK, CHUNK)
         short_copies[2 * chunks + q].wait_recv()
@@ -352,7 +348,7 @@
             pltpu.SemaphoreType.DMA((2,)),
         ],
         compiler_params=pltpu.CompilerParams(
-            collective_id=0, has_side_effects=True, vmem_limit_bytes=56 * 1024 * 1024
+            collective_id=0, has_side_effects=True, vmem_limit_bytes=53 * 1024 * 1024
         ),
         name="grape",
     )(propagators[0, 0], target, weights)

time: 71.8 us -> 70.2 us (0.978)
  local copies, waits for them, and re-layouts: 1.69 us -> 0.79 us
    broadcast_in_dim x1, local copies, waits for them, and re-layouts: 1.69 us -> 0.79 us  [shards(): return summed[:, None, :]]
where the time goes in v4:
time: 70.2 us
  Pallas kernels  68.7 us (98%)
  local copies, waits for them, and re-layouts  0.79 us (1%)
    pallas_call x1, Pallas kernels, shards(): pl.pallas_call(kernel, out_shape=jax.ShapeDtypeStruct((ROWS, R), jnp.floa...  68.7 us

profile of v4, /device:TPU:32, one launch (start us, length us, event | category | flops | bytes accessed | tf_op | source)
XLA Modules:
  0.0 70.2 jit_solution(3349531677172710701)
XLA Ops:
  0.7 68.7 %grape.1 = f32[64,512]{1,0:T(8,128)S(1)} custom-call(f32[512,512]{1,0:T(8,128)} %bitcast.3, f32[512,512]{1,0:T(8,128)} %target_ref.1, f32[1]{0:T(128)S(6)} %copy.5.weight_ref), custom_call_target="tpu_custom_call" | custom-call | tf_op jit(solution)/shard_map/grape/pallas_call | solution.py:326
  69.4 0.8 %copy.4 = f32[64,1,512]{2,1,0:T(1,128)} copy(f32[64,1,512]{2,0,1:T(8,128)S(1)} %bitcast.2) | data formatting | bytes 262144 | tf_op jit(solution)/shard_map/broadcast_in_dim | solution.py:355

commit v5 on v4

--- a/solution.py
+++ b/solution.py
@@ -14,7 +14,7 @@
 SMALL = 64
 SUB = 32
 ROWS = 64
-CHUNK = 16
+CHUNK = 8
 COPIES = 160
 
 
@@ -69,12 +69,12 @@
         started.append(copy)
         return copy
 
-    def prepare(b):
+    def prepare(b, spot=0):
         high, low = split(b[...])
-        bh[...] = high
-        bl[...] = low
-
-    def product_rows(dst, a, start, count, nt=False):
+        bh[spot] = high
+        bl[spot] = low
+
+    def product_rows(dst, a, start, count, nt=False, spot=0):
         dims = (((1,), (1 if nt else 0,)), ((), ()))
 
         def dot(p, q):
@@ -82,7 +82,7 @@
 
         block = pl.ds(start, count)
         high, low = split(a[block, :])
-        dst[block, :] = dot(high, bh[...]) + (dot(high, bl[...]) + dot(low, bh[...]))
+        dst[block, :] = dot(high, bh[spot]) + (dot(high, bl[spot]) + dot(low, bh[spot]))
 
     def product(dst, a, b, nt=False):
         prepare(b)
@@ -142,6 +142,31 @@
     def _():
         product(ends.at[2], ends.at[0], mats.at[2 * late])
 
+    subs = SMALL // SUB
+
+    def pieces(half, number):
+        start = half * HALF + number * SMALL
+        return [pl.ds(pl.multiple_of(start + n * SUB, SUB), SUB) for n in range(subs)]
+
+    a_here, b_here = pieces(odd, core), pieces(odd, 2 + core)
+    a_there, b_there = pieces(1 - odd, core), pieces(1 - odd, 2 + core)
+    begin = mats.at[3 + 2 * late]
+    third = y == 2
+
+    def gather_strip():
+        for n in range(subs):
+            strip[n * SUB:(n + 1) * SUB, :] = begin[a_here[n], :]
+            strip[SMALL + n * SUB:SMALL + (n + 1) * SUB, :] = begin[b_here[n], :]
+
+    prepare(mats.at[(1 - late) * 4 + late * (1 - odd)], 1)
+    target_load.wait()
+    prepare(target, 2)
+
+    @pl.when(third)
+    def _():
+        gather_strip()
+        product_rows(strip, strip, 0, 2 * SMALL, spot=1)
+
     up2.wait_recv()
     far = [pass_on(mats.at[yo], first)]
     down2.wait_recv()
@@ -149,28 +174,21 @@
     for copy in far:
         copy.wait_recv()
 
-    subs = SMALL // SUB
-
-    def pieces(half, number):
-        start = half * HALF + number * SMALL
-        return [pl.ds(pl.multiple_of(start + n * SUB, SUB), SUB) for n in range(subs)]
-
-    a_here, b_here = pieces(odd, core), pieces(odd, 2 + core)
-    a_there, b_there = pieces(1 - odd, core), pieces(1 - odd, 2 + core)
-    begin = mats.at[3 + 2 * late]
-    for n in range(subs):
-        strip[n * SUB:(n + 1) * SUB, :] = begin[a_here[n], :]
-        strip[SMALL + n * SUB:SMALL + (n + 1) * SUB, :] = begin[b_here[n], :]
-    prepare(mats.at[2 - late])
-    product_rows(strip, strip, 0, 2 * SMALL)
-    prepare(mats.at[4 - 4 * late])
-    product_rows(strip, strip, 0, 2 * SMALL)
-    target_load.wait()
+    @pl.when(third)
+    def _():
+        prepare(mats.at[0])
+        product_rows(strip, strip, 0, 2 * SMALL)
+
+    @pl.when(jnp.logical_not(third))
+    def _():
+        prepare(mats.at[2 - late])
+        gather_strip()
+        product_rows(strip, strip, 0, 2 * SMALL)
+        product_rows(strip, strip, 0, 2 * SMALL, spot=1)
 
     @pl.when(x == 0)
     def _():
-        prepare(target)
-        product_rows(strip, strip, 0, 2 * SMALL, nt=True)
+        product_rows(strip, strip, 0, 2 * SMALL, nt=True, spot=2)
 
     strip_a = [strip.at[pl.ds(n * SUB, SUB)] for n in range(subs)]
     strip_b = [strip.at[pl.ds(SMALL + n * SUB, SUB)] for n in range(subs)]
@@ -341,8 +359,8 @@
             full, full, full, full, full,
             pltpu.VMEM((4, ROWS, R), jnp.float32),
             pltpu.VMEM((3, ROWS, R), jnp.float32),
-            pltpu.VMEM((R, R), jnp.bfloat16),
-            pltpu.VMEM((R, R), jnp.bfloat16),
+            pltpu.VMEM((3, R, R), jnp.bfloat16),
+            pltpu.VMEM((3, R, R), jnp.bfloat16),
             pltpu.SemaphoreType.DMA((COPIES,)),
             pltpu.SemaphoreType.DMA((COPIES,)),
             pltpu.SemaphoreType.DMA((2,)),

time: 70.2 us -> 69.9 us (level)
  no operation moved by 1% of the time
where the time goes in v5:
time: 69.9 us; the launch traced here: 69.8 us
  Pallas kernels  68.4 us (98%)
  local copies, waits for them, and re-layouts  0.79 us (1%)
    pallas_call x1, Pallas kernels, shards(): pl.pallas_call(kernel, out_shape=jax.ShapeDtypeStruct((ROWS, R), jnp.floa...  68.4 us

profile of v5, /device:TPU:32, one launch (start us, length us, event | category | flops | bytes accessed | tf_op | source)
XLA Modules:
  0.0 69.8 jit_solution(7731579458222599960)
XLA Ops:
  0.7 68.4 %grape.1 = f32[64,512]{1,0:T(8,128)S(1)} custom-call(f32[512,512]{1,0:T(8,128)} %bitcast.3, f32[512,512]{1,0:T(8,128)} %target_ref.1, f32[1]{0:T(128)S(6)} %copy.5.weight_ref), custom_call_target="tpu_custom_call" | custom-call | tf_op jit(solution)/shard_map/grape/pallas_call | solution.py:344
  69.0 0.8 %copy.4 = f32[64,1,512]{2,1,0:T(1,128)} copy(f32[64,1,512]{2,0,1:T(8,128)S(1)} %bitcast.2) | data formatting | bytes 262144 | tf_op jit(solution)/shard_map/broadcast_in_dim | solution.py:373

commit v6 on v5

--- a/solution.py
+++ b/solution.py
@@ -49,7 +49,6 @@
     own_load = pltpu.make_async_copy(prop_ref, ends.at[core], local_sem.at[0])
     own_load.start()
     target_load = pltpu.make_async_copy(target_ref, target, local_sem.at[1])
-    target_load.start()
 
     barrier = pltpu.get_barrier_semaphore()
     peers = (sibling, to_yp, to_ym, to_xp, to_xm, to_long, to_short)
@@ -96,6 +95,7 @@
     swap = send(prop_ref, ends.at[core], sibling)
     own_load.wait()
     swap.wait_recv()
+    target_load.start()
     mine = pl.multiple_of(core * HALF, HALF)
     other = pl.multiple_of((1 - core) * HALF, HALF)
     first, second = pl.ds(mine, PIECE), pl.ds(mine + PIECE, PIECE)

time: 69.9 us -> 69.9 us (level)
  no operation moved by 1% of the time
where the time goes in v6:
time: 69.9 us; the launch traced here: 69.8 us
  Pallas kernels  68.4 us (98%)
  local copies, waits for them, and re-layouts  0.79 us (1%)
    pallas_call x1, Pallas kernels, shards(): pl.pallas_call(kernel, out_shape=jax.ShapeDtypeStruct((ROWS, R), jnp.floa...  68.4 us

profile of v6, /device:TPU:32, one launch (start us, length us, event | category | flops | bytes accessed | tf_op | source)
XLA Modules:
  0.0 69.8 jit_solution(8492979093971304448)
XLA Ops:
  0.7 68.4 %grape.1 = f32[64,512]{1,0:T(8,128)S(1)} custom-call(f32[512,512]{1,0:T(8,128)} %bitcast.3, f32[512,512]{1,0:T(8,128)} %target_ref.1, f32[1]{0:T(128)S(6)} %copy.5.weight_ref), custom_call_target="tpu_custom_call" | custom-call | tf_op jit(solution)/shard_map/grape/pallas_call | solution.py:344
  69.0 0.8 %copy.4 = f32[64,1,512]{2,1,0:T(1,128)} copy(f32[64,1,512]{2,0,1:T(8,128)S(1)} %bitcast.2) | data formatting | bytes 262144 | tf_op jit(solution)/shard_map/broadcast_in_dim | solution.py:373
